TPU v7x, 32 devices: a whole 2x2x4 slice. The times are simulated.
32 devices in a mesh: pair: 8 (over z, x), row: 4 (over y, core).
Axes of the slice: x: 2, y: 2, z: 4, core: 2. Of those that a mesh axis runs over, the one named last changes fastest.
Arguments:
- sector: float32 [8192, 2048], P('row', 'pair'), may hold values from -1.767767 to 1.767767
- block_label: int32 [16], replicated, may hold values from 0 to 15, each once
Outputs:
- rotated: float32 [8192, 2048], P('row', 'pair')
- vectors: float32 [2048, 2048], P('row', 'pair')
- singular: float32 [2048], P('pair')
Inputs may be any that keep to these rules, and one draw needn't show every extreme that they name: `block_label`: each block number appears once.
All inputs are finite; a program needn't handle non-finite values.
Results may differ from a plain program's by a relative error of at most 0.0003.
Values sent between devices are 32-bit elements; how exact they have to be, the bound alone decides.
No kernel may reach another device: no remote copies, remote signals or barrier semaphores. Data moves between devices by JAX's collectives and lax.ppermute only.
A program may use at most 64 MiB of HBM per device.

v0:
```python
import jax
import jax.numpy as jnp
from jax import lax
from jax.sharding import PartitionSpec as P

ROUNDS = 4
NEWTON = 16
highest = lax.Precision.HIGHEST


def from_behind(block, axis, distance):
    devices = range(lax.axis_size(axis))
    route = [(i - distance, i) for i in devices if i - distance in devices]
    return lax.ppermute(block, axis, route)


def rotation_of(gram_matrix):
    size_two = gram_matrix.shape[0]
    diagonal = jnp.diagonal(gram_matrix)
    spread = diagonal[None, :] - diagonal[:, None]
    summed = diagonal[None, :] + diagonal[:, None]
    skewed = (
        gram_matrix
        * spread
        / (spread * spread + 2.0 * gram_matrix * gram_matrix + 0.01 * summed * summed)
    )
    identity = jnp.eye(size_two, dtype=jnp.float32)
    half_step = identity + 0.5 * skewed
    system = identity - 0.25 * jnp.dot(skewed, skewed, precision=highest)
    bound = 1.0 + 0.25 * jnp.sum(skewed * skewed)
    inverse = 2.0 / (1.0 + bound) * identity
    for newton_step in range(NEWTON):
        inverse = jnp.dot(
            inverse, 2.0 * identity - jnp.dot(system, inverse, precision=highest), precision=highest
        )
    return jnp.dot(inverse, jnp.dot(half_step, half_step, precision=highest), precision=highest)


def send_leftward(moving):
    return from_behind(moving, "pair", -1)


def send_rightward(moving):
    return from_behind(moving, "pair", 1)


def per_device(sector, block_label):
    local_rows = sector.shape[0]
    width_pair = sector.shape[1]
    half_width = width_pair // 2
    pair_count = lax.axis_size("pair")
    position = lax.axis_index("pair")
    row_index = lax.axis_index("row")
    vector_rows = pair_count * width_pair // lax.axis_size("row")
    labels = lax.dynamic_slice_in_dim(block_label, 2 * position, 2)
    targets = (
        labels[:, None] * half_width + jnp.arange(half_width, dtype=jnp.int32)[None, :]
    ).reshape(width_pair)
    row_ids = row_index * vector_rows + jnp.arange(vector_rows, dtype=jnp.int32)
    vectors = (row_ids[:, None] == targets[None, :]).astype(jnp.float32)
    stacked = jnp.concatenate([sector, vectors], 0)
    is_first = position == 0
    is_last = position == pair_count - 1
    for sweep_round in range(ROUNDS):
        columns = stacked[:local_rows]
        gram_matrix = lax.psum(jnp.dot(columns.T, columns, precision=highest), "row")
        rotation = rotation_of(gram_matrix)
        if sweep_round == ROUNDS - 1:
            stacked = jnp.dot(stacked, rotation, precision=highest)
        else:
            turned = jnp.dot(stacked, rotation, precision=highest)
            upper_half = turned[:, :half_width]
            lower_half = turned[:, half_width:]
            from_right = send_leftward(lower_half)
            from_left = send_rightward(jnp.where(is_first, lower_half, upper_half))
            new_upper = jnp.where(is_first, upper_half, from_left)
            new_lower = jnp.where(is_last, upper_half, from_right)
            stacked = jnp.concatenate([new_upper, new_lower], 1)
    rotated = stacked[:local_rows]
    vectors_out = stacked[local_rows:]
    squares = lax.psum(jnp.sum(rotated * rotated, axis=0), "row")
    singular = jnp.sqrt(squares + 1e-06)
    return (rotated, vectors_out, singular)


def solution(mesh):
    placed = (P("row", "pair"), P())
    return jax.shard_map(
        per_device,
        mesh=mesh,
        in_specs=placed,
        out_specs=(P("row", "pair"), P("row", "pair"), P("pair")),
        check_vma=False,
    )
```

profile of v0, /device:TPU:0, one launch (start us, length us, event | category | flops | bytes accessed | tf_op | source)
XLA Modules:
  0.0 438.3 jit_solution(17083182142614953925)
XLA Ops:
  7.2 6.4 %fusion.107 = f32[256,256]{1,0:T(8,128)} fusion(f32[2048,256]{1,0:T(8,128)} %param.2), kind=kOutput, calls=%fused_computation.216 | convolution fusion | flops 1610612736 | bytes 2359296 | tf_op jit(solution)/shard_map/dot_general | solution.py:66
  14.2 34.3 %all-reduce.5.cloned.1.call-done = f32[256,256]{1,0:T(8,128)} async-done(((f32[256,256]{1,0:T(8,128)}), f32[256,256]{1,0:T(8,128)}) %all-reduce.5.cloned.1.call-update) | async-done | bytes 262160 | tf_op jit(solution)/shard_map/psum | solution.py:66
  48.5 2.6 gather_fusion
  51.1 0.8 multiply_reduce_fusion.4
  66.8 2.6 fusion
  69.4 1.7 slice_select_fusion.8
  71.1 4.4 %collective-permute-start = (f32[2560,128]{0,1:T(8,128)}, f32[2560,128]{0,1:T(8,128)}, u32[]{:S(2)}, u32[]{:S(2)}) collective-permute-start(f32[2560,128]{0,1:T(8,128)} %get-tuple-element.23), channel_id=1, source_target_pairs={{0,4},{4,8},{8,12},{12,16},{16,20},{20,24},{24,28},{1,5},{5,9},{9,... | collective-permute-start | bytes 3932168 | tf_op jit(solution)/shard_map/ppermute | solution.py:14
  75.6 1.3 collective-permute-start.1
  76.9 52.9 %collective-permute-done = f32[2560,128]{0,1:T(8,128)} collective-permute-done((f32[2560,128]{0,1:T(8,128)}, f32[2560,128]{0,1:T(8,128)}, u32[]{:S(2)}, u32[]{:S(2)}) %collective-permute-start) | collective-permute-done | bytes 1310752 | tf_op jit(solution)/shard_map/ppermute | solution.py:14
  129.8 1.7 slice_select_fusion.7
  131.5 1.1 copy-done.1
  133.0 2.6 fusion.24
  136.1 33.4 %all-reduce.7.cloned.1.call-done = f32[256,256]{1,0:T(8,128)} async-done(((f32[256,256]{1,0:T(8,128)}), f32[256,256]{1,0:T(8,128)}) %all-reduce.7.cloned.1.call-update) | async-done | bytes 262160 | tf_op jit(solution)/shard_map/psum | solution.py:66
  169.5 2.6 gather_fusion.1
  187.6 2.6 fusion.4
  190.4 3.5 collective-permute-start.2
  193.9 1.3 collective-permute-start.3
  195.2 53.6 %collective-permute-done.2 = f32[2560,128]{0,1:T(8,128)S(1)} collective-permute-done((f32[2560,128]{0,1:T(8,128)S(1)}, f32[2560,128]{0,1:T(8,128)S(1)}, u32[]{:S(2)}, u32[]{:S(2)}) %collective-permute-start.2) | collective-permute-done | bytes 1310752 | tf_op jit(solution)/shard_map/ppermute | solution.py:14
  249.0 2.6 fusion.20
  252.1 33.0 %all-reduce.9.cloned.1.call-done = f32[256,256]{1,0:T(8,128)} async-done(((f32[256,256]{1,0:T(8,128)}), f32[256,256]{1,0:T(8,128)}) %all-reduce.9.cloned.1.call-update) | async-done | bytes 262160 | tf_op jit(solution)/shard_map/psum | solution.py:66
  285.0 2.6 gather_fusion.2
  302.9 2.6 fusion.8
  305.7 3.5 collective-permute-start.4
  309.2 1.3 collective-permute-start.5
  310.5 53.6 %collective-permute-done.4 = f32[2560,128]{0,1:T(8,128)S(1)} collective-permute-done((f32[2560,128]{0,1:T(8,128)S(1)}, f32[2560,128]{0,1:T(8,128)S(1)}, u32[]{:S(2)}, u32[]{:S(2)}) %collective-permute-start.4) | collective-permute-done | bytes 1310752 | tf_op jit(solution)/shard_map/ppermute | solution.py:14
  364.3 2.6 fusion.16
  366.9 33.4 %all-reduce.11.cloned.1.call-done = f32[256,256]{1,0:T(8,128)} async-done(((f32[256,256]{1,0:T(8,128)}), f32[256,256]{1,0:T(8,128)}) %all-reduce.11.cloned.1.call-update) | async-done | bytes 262160 | tf_op jit(solution)/shard_map/psum | solution.py:66
  400.4 2.6 gather_fusion.3
  418.2 4.6 %fusion.12 = f32[2560,256]{1,0:T(8,128)S(1)} fusion(f32[256,256]{1,0:T(8,128)S(1)} %fusion.171, f32[2560,128]{0,1:T(8,128)S(1)} %get-tuple-element.14, f32[2560,128]{0,1:T(8,128)S(1)} %get-tuple-element.13), kind=kOutput, calls=%fused_computation.80 | convolution fusion | flops 2013921280 | bytes 5505024 | tf_op jit(solution)/shard_map/dot_general | solution.py:69
  422.8 0.8 slice.59
  423.6 1.6 multiply_reduce_fusion
  425.2 5.7 %psum.39 = f32[256]{0:T(256)S(1)} all-reduce(f32[256]{0:T(256)S(1)} %get-tuple-element.3), channel_id=1, replica_groups=mesh['pair'=8,'row'=4] {'row'}, use_global_device_ids=true, to_apply=%region_9.10 | all-reduce | flops 256 | bytes 2048 | tf_op jit(solution)/shard_map/psum | solution.py:81
  (183 shorter events, 60.3 us)
Async XLA Ops:
  7.2 6.7 %copy-start.9 = (s32[16]{0:T(128)S(1)}, s32[16]{0:T(128)}, u32[]{:S(2)}) copy-start(s32[16]{0:T(128)} %param.3) | copy-start | bytes 196
  7.2 41.3 %all-reduce.5.cloned.1.call-start = ((), (), s32[]{:S(2)}) async-start(), calls=%async_computation | async-start | bytes 524288 | tf_op jit(solution)/shard_map/psum | solution.py:66
  13.6 155.8 %all-reduce.7.cloned.1.call-start = ((), (), s32[]{:S(2)}) async-start(), calls=%async_computation.1 | async-start | bytes 524288 | tf_op jit(solution)/shard_map/psum | solution.py:66
  48.5 2.6 copy-start.5
  65.2 1.6 copy-start
  71.1 58.7 %collective-permute-start = (f32[2560,128]{0,1:T(8,128)}, f32[2560,128]{0,1:T(8,128)}, u32[]{:S(2)}, u32[]{:S(2)}) collective-permute-start(f32[2560,128]{0,1:T(8,128)} %get-tuple-element.23), channel_id=1, source_target_pairs={{0,4},{4,8},{8,12},{12,16},{16,20},{20,24},{24,28},{1,5},{5,9},{9,... | collective-permute-start | bytes 3932168 | tf_op jit(solution)/shard_map/ppermute | solution.py:14
  75.6 54.2 %collective-permute-start.1 = (f32[2560,128]{0,1:T(8,128)}, f32[2560,128]{0,1:T(8,128)}, u32[]{:S(2)}, u32[]{:S(2)}) collective-permute-start(f32[2560,128]{0,1:T(8,128)} %get-tuple-element.24), channel_id=1, source_target_pairs={{4,0},{8,4},{12,8},{16,12},{20,16},{24,20},{28,24},{5,1},{9,5},{13... | collective-permute-start | bytes 3932168 | tf_op jit(solution)/shard_map/ppermute | solution.py:14
  131.5 1.1 copy-start.1
  131.5 1.5 copy-start.3
  135.6 149.4 %all-reduce.9.cloned.1.call-start = ((), (), s32[]{:S(2)}) async-start(), calls=%async_computation.2 | async-start | bytes 524288 | tf_op jit(solution)/shard_map/psum | solution.py:66
  169.5 2.6 copy-start.6
  185.8 1.6 copy-start.4
  186.2 1.4 copy-start.2
  190.4 58.4 %collective-permute-start.2 = (f32[2560,128]{0,1:T(8,128)S(1)}, f32[2560,128]{0,1:T(8,128)S(1)}, u32[]{:S(2)}, u32[]{:S(2)}) collective-permute-start(f32[2560,128]{0,1:T(8,128)S(1)} %get-tuple-element.19), channel_id=1, source_target_pairs={{0,4},{4,8},{8,12},{12,16},{16,20},{20,24},{24,28},{1,5},{5,9},{9,... | collective-permute-start | bytes 3932168 | tf_op jit(solution)/shard_map/ppermute | solution.py:14
  193.9 54.9 %collective-permute-start.3 = (f32[2560,128]{0,1:T(8,128)S(1)}, f32[2560,128]{0,1:T(8,128)S(1)}, u32[]{:S(2)}, u32[]{:S(2)}) collective-permute-start(f32[2560,128]{0,1:T(8,128)S(1)} %get-tuple-element.20), channel_id=1, source_target_pairs={{4,0},{8,4},{12,8},{16,12},{20,16},{24,20},{28,24},{5,1},{9,5},{13... | collective-permute-start | bytes 3932168 | tf_op jit(solution)/shard_map/ppermute | solution.py:14
  251.6 148.8 %all-reduce.11.cloned.1.call-start = ((), (), s32[]{:S(2)}) async-start(), calls=%async_computation.3 | async-start | bytes 524288 | tf_op jit(solution)/shard_map/psum | solution.py:66
  285.0 2.6 copy-start.7
  305.7 58.4 %collective-permute-start.4 = (f32[2560,128]{0,1:T(8,128)S(1)}, f32[2560,128]{0,1:T(8,128)S(1)}, u32[]{:S(2)}, u32[]{:S(2)}) collective-permute-start(f32[2560,128]{0,1:T(8,128)S(1)} %get-tuple-element.15), channel_id=1, source_target_pairs={{0,4},{4,8},{8,12},{12,16},{16,20},{20,24},{24,28},{1,5},{5,9},{9,... | collective-permute-start | bytes 3932168 | tf_op jit(solution)/shard_map/ppermute | solution.py:14
  309.2 54.9 %collective-permute-start.5 = (f32[2560,128]{0,1:T(8,128)S(1)}, f32[2560,128]{0,1:T(8,128)S(1)}, u32[]{:S(2)}, u32[]{:S(2)}) collective-permute-start(f32[2560,128]{0,1:T(8,128)S(1)} %get-tuple-element.16), channel_id=1, source_target_pairs={{4,0},{8,4},{12,8},{16,12},{20,16},{24,20},{28,24},{5,1},{9,5},{13... | collective-permute-start | bytes 3932168 | tf_op jit(solution)/shard_map/ppermute | solution.py:14
  400.4 2.6 copy-start.8
Sparse Core Ops, SparseCore 0:
  13.8 34.6 all-reduce.4
  135.7 33.6 all-reduce.6
  251.7 33.2 all-reduce.8
  367.0 33.2 all-reduce.10
where the time goes:
time: 442 us; the launch traced here: 438 us
  waiting for transfers between devices  294 us (67%)
  matrix products  80.3 us (18%)
  between operations  18.1 us (4%)
  starting transfers between devices  16.4 us (4%)
  local copies, waits for them, and re-layouts  13.6 us (3%)
  other arithmetic  9.97 us (2%)
  blocking collectives  5.73 us (1%)
    ppermute x6, waiting for transfers between devices, from_behind(): return lax.ppermute(block, axis, route)  160 us
    psum x4, waiting for transfers between devices, per_device(): lax.psum(jnp.dot(columns.T, columns, precision=highest), 'row')  134 us
    dot_general x64, matrix products, rotation_of(): jnp.dot(inverse, 2.0 * identity - jnp.dot(system, inverse, precision=high...  24.9 us
    dot_general x64, matrix products, rotation_of(): jnp.dot(system, inverse, precision=highest)  24.2 us
    ppermute x6, starting transfers between devices, from_behind(): return lax.ppermute(block, axis, route)  15.2 us
    dot_general x4, matrix products, per_device(): jnp.dot(columns.T, columns, precision=highest)  14.1 us
    gather x4, local copies, waits for them, and re-layouts, rotation_of(): diagonal = jnp.diagonal(gram_matrix)  10.5 us
  transfers between devices with their start and end apart: 10, of which 7 were waited for; matrix products, arithmetic and copies ran while one was open for 0% of the time, Pallas kernels for 0%

commit v1 on v0

--- a/solution.py
+++ b/solution.py
@@ -63,7 +63,9 @@
     is_last = position == pair_count - 1
     for sweep_round in range(ROUNDS):
         columns = stacked[:local_rows]
-        gram_matrix = lax.psum(jnp.dot(columns.T, columns, precision=highest), "row")
+        gram_matrix = jnp.sum(
+            lax.all_gather(jnp.dot(columns.T, columns, precision=highest), "row"), axis=0
+        )
         rotation = rotation_of(gram_matrix)
         if sweep_round == ROUNDS - 1:
             stacked = jnp.dot(stacked, rotation, precision=highest)

time: 442 us -> 390 us (0.88)
  waiting for transfers between devices: 294 us -> 238 us
  other arithmetic: 9.97 us -> 15.2 us
    psum x4 -> x0, waiting for transfers between devices: 134 us -> none  [per_device(): lax.psum(jnp.dot(columns.T, columns, precision=highest), 'row')]
    all_gather x0 -> x4, waiting for transfers between devices: none -> 73.2 us  [per_device(): lax.all_gather(jnp.dot(columns.T, columns, precision=highest), 'row')]
    reduce_sum x0 -> x4, other arithmetic: none -> 5.31 us  [per_device(): jnp.sum(lax.all_gather(jnp.dot(columns.T, columns, precision=highest), 'r...]
    ppermute x6, waiting for transfers between devices: 160 us -> 165 us  [from_behind(): return lax.ppermute(block, axis, route)]
where the time goes in v1:
time: 390 us; the launch traced here: 386 us
  waiting for transfers between devices  238 us (61%)
  matrix products  80.5 us (21%)
  between operations  18.1 us (5%)
  starting transfers between devices  15.4 us (4%)
  other arithmetic  15.2 us (4%)
  local copies, waits for them, and re-layouts  13 us (3%)
  blocking collectives  5.86 us (2%)
    ppermute x6, waiting for transfers between devices, from_behind(): return lax.ppermute(block, axis, route)  165 us
    all_gather x4, waiting for transfers between devices, per_device(): lax.all_gather(jnp.dot(columns.T, columns, precision=highest), 'row')  73.2 us
    dot_general x64, matrix products, rotation_of(): jnp.dot(system, inverse, precision=highest)  25.2 us
    dot_general x64, matrix products, rotation_of(): jnp.dot(inverse, 2.0 * identity - jnp.dot(system, inverse, precision=high...  24.1 us
    ppermute x6, starting transfers between devices, from_behind(): return lax.ppermute(block, axis, route)  15.2 us
    dot_general x4, matrix products, per_device(): jnp.dot(columns.T, columns, precision=highest)  14.1 us
    gather x4, local copies, waits for them, and re-layouts, rotation_of(): diagonal = jnp.diagonal(gram_matrix)  10.5 us
    dot_general x3, matrix products, per_device(): turned = jnp.dot(stacked, rotation, precision=highest)  7.87 us
  transfers between devices with their start and end apart: 10, of which 7 were waited for; matrix products, arithmetic and copies ran while one was open for 0% of the time, Pallas kernels for 0%

profile of v1, /device:TPU:0, one launch (start us, length us, event | category | flops | bytes accessed | tf_op | source)
XLA Modules:
  0.0 386.0 jit_solution(17600428581968654523)
XLA Ops:
  7.2 6.4 %fusion.107 = f32[256,256]{1,0:T(8,128)} fusion(f32[2048,256]{1,0:T(8,128)} %param.2), kind=kOutput, calls=%fused_computation.216 | convolution fusion | flops 1610612736 | bytes 2359296 | tf_op jit(solution)/shard_map/dot_general | solution.py:67
  14.0 19.2 %all-gather.9.cloned.1.call-done = f32[1024,256]{1,0:T(8,128)} async-done(((f32[256,256]{1,0:T(8,128)}), f32[1024,256]{1,0:T(8,128)}) %all-gather.9.cloned.1.call-update) | async-done | bytes 1048592 | tf_op jit(solution)/shard_map/all_gather | solution.py:67
  33.2 1.3 reduce_sum.81
  34.5 2.9 gather_fusion
  52.9 2.6 fusion
  55.5 1.7 slice_select_fusion.8
  57.2 4.4 %collective-permute-start = (f32[2560,128]{0,1:T(8,128)}, f32[2560,128]{0,1:T(8,128)}, u32[]{:S(2)}, u32[]{:S(2)}) collective-permute-start(f32[2560,128]{0,1:T(8,128)} %get-tuple-element.23), channel_id=1, source_target_pairs={{0,4},{4,8},{8,12},{12,16},{16,20},{20,24},{24,28},{1,5},{5,9},{9,... | collective-permute-start | bytes 3932168 | tf_op jit(solution)/shard_map/ppermute | solution.py:14
  62.9 54.5 %collective-permute-done = f32[2560,128]{0,1:T(8,128)} collective-permute-done((f32[2560,128]{0,1:T(8,128)}, f32[2560,128]{0,1:T(8,128)}, u32[]{:S(2)}, u32[]{:S(2)}) %collective-permute-start) | collective-permute-done | bytes 1310752 | tf_op jit(solution)/shard_map/ppermute | solution.py:14
  117.4 1.7 slice_select_fusion.7
  120.6 2.6 fusion.24
  123.2 18.2 %all-gather.11.cloned.1.call-done = f32[1024,256]{1,0:T(8,128)} async-done(((f32[256,256]{1,0:T(8,128)}), f32[1024,256]{1,0:T(8,128)}) %all-gather.11.cloned.1.call-update) | async-done | bytes 1048592 | tf_op jit(solution)/shard_map/all_gather | solution.py:67
  141.5 1.3 reduce_sum.83
  142.8 2.3 gather_fusion.1
  160.6 2.6 fusion.4
  163.5 3.5 collective-permute-start.2
  166.9 1.3 collective-permute-start.3
  168.2 55.1 %collective-permute-done.2 = f32[2560,128]{0,1:T(8,128)S(1)} collective-permute-done((f32[2560,128]{0,1:T(8,128)S(1)}, f32[2560,128]{0,1:T(8,128)S(1)}, u32[]{:S(2)}, u32[]{:S(2)}) %collective-permute-start.2) | collective-permute-done | bytes 1310752 | tf_op jit(solution)/shard_map/ppermute | solution.py:14
  223.6 2.6 fusion.20
  226.2 17.8 %all-gather.13.cloned.1.call-done = f32[1024,256]{1,0:T(8,128)} async-done(((f32[256,256]{1,0:T(8,128)}), f32[1024,256]{1,0:T(8,128)}) %all-gather.13.cloned.1.call-update) | async-done | bytes 1048592 | tf_op jit(solution)/shard_map/all_gather | solution.py:67
  244.1 1.3 reduce_sum.85
  245.4 2.5 gather_fusion.2
  263.2 2.6 fusion.8
  266.0 3.5 collective-permute-start.4
  269.5 1.3 collective-permute-start.5
  270.8 55.1 %collective-permute-done.4 = f32[2560,128]{0,1:T(8,128)S(1)} collective-permute-done((f32[2560,128]{0,1:T(8,128)S(1)}, f32[2560,128]{0,1:T(8,128)S(1)}, u32[]{:S(2)}, u32[]{:S(2)}) %collective-permute-start.4) | collective-permute-done | bytes 1310752 | tf_op jit(solution)/shard_map/ppermute | solution.py:14
  326.1 2.6 fusion.16
  328.7 17.9 %all-gather.15.cloned.1.call-done = f32[1024,256]{1,0:T(8,128)} async-done(((f32[256,256]{1,0:T(8,128)}), f32[1024,256]{1,0:T(8,128)}) %all-gather.15.cloned.1.call-update) | async-done | bytes 1048592 | tf_op jit(solution)/shard_map/all_gather | solution.py:67
  346.6 1.3 reduce_sum.87
  348.0 2.7 gather_fusion.3
  365.9 4.6 %fusion.12 = f32[2560,256]{1,0:T(8,128)S(1)} fusion(f32[256,256]{1,0:T(8,128)S(1)} %fusion.171, f32[2560,128]{0,1:T(8,128)S(1)} %get-tuple-element.14, f32[2560,128]{0,1:T(8,128)S(1)} %get-tuple-element.13), kind=kOutput, calls=%fused_computation.80 | convolution fusion | flops 2013921280 | bytes 5505024 | tf_op jit(solution)/shard_map/dot_general | solution.py:71
  371.3 1.6 multiply_reduce_fusion
  372.9 5.9 %psum.7 = f32[256]{0:T(256)S(1)} all-reduce(f32[256]{0:T(256)S(1)} %get-tuple-element.3), channel_id=1, replica_groups=mesh['pair'=8,'row'=4] {'row'}, use_global_device_ids=true, to_apply=%region_9.10 | all-reduce | flops 256 | bytes 2048 | tf_op jit(solution)/shard_map/psum | solution.py:83
  (179 shorter events, 63.0 us)
Async XLA Ops:
  7.2 6.5 %copy-start.5 = (s32[16]{0:T(128)S(1)}, s32[16]{0:T(128)}, u32[]{:S(2)}) copy-start(s32[16]{0:T(128)} %param.3) | copy-start | bytes 196
  7.2 26.0 %all-gather.9.cloned.1.call-start = ((), (), s32[]{:S(2)}) async-start(), calls=%async_computation | async-start | bytes 1310720 | tf_op jit(solution)/shard_map/all_gather | solution.py:67
  13.6 127.8 %all-gather.11.cloned.1.call-start = ((), (), s32[]{:S(2)}) async-start(), calls=%async_computation.1 | async-start | bytes 1310720 | tf_op jit(solution)/shard_map/all_gather | solution.py:67
  51.3 1.6 copy-start
  57.2 60.2 %collective-permute-start = (f32[2560,128]{0,1:T(8,128)}, f32[2560,128]{0,1:T(8,128)}, u32[]{:S(2)}, u32[]{:S(2)}) collective-permute-start(f32[2560,128]{0,1:T(8,128)} %get-tuple-element.23), channel_id=1, source_target_pairs={{0,4},{4,8},{8,12},{12,16},{16,20},{20,24},{24,28},{1,5},{5,9},{9,... | collective-permute-start | bytes 3932168 | tf_op jit(solution)/shard_map/ppermute | solution.py:14
  61.6 55.8 %collective-permute-start.1 = (f32[2560,128]{0,1:T(8,128)}, f32[2560,128]{0,1:T(8,128)}, u32[]{:S(2)}, u32[]{:S(2)}) collective-permute-start(f32[2560,128]{0,1:T(8,128)} %get-tuple-element.24), channel_id=1, source_target_pairs={{4,0},{8,4},{12,8},{16,12},{20,16},{24,20},{28,24},{5,1},{9,5},{13... | collective-permute-start | bytes 3932168 | tf_op jit(solution)/shard_map/ppermute | solution.py:14
  119.1 1.1 copy-start.1
  119.1 1.5 copy-start.3
  123.2 120.9 %all-gather.13.cloned.1.call-start = ((), (), s32[]{:S(2)}) async-start(), calls=%async_computation.2 | async-start | bytes 1310720 | tf_op jit(solution)/shard_map/all_gather | solution.py:67
  158.6 2.0 copy-start.4
  159.0 1.6 copy-start.2
  163.5 59.9 %collective-permute-start.2 = (f32[2560,128]{0,1:T(8,128)S(1)}, f32[2560,128]{0,1:T(8,128)S(1)}, u32[]{:S(2)}, u32[]{:S(2)}) collective-permute-start(f32[2560,128]{0,1:T(8,128)S(1)} %get-tuple-element.19), channel_id=1, source_target_pairs={{0,4},{4,8},{8,12},{12,16},{16,20},{20,24},{24,28},{1,5},{5,9},{9,... | collective-permute-start | bytes 3932168 | tf_op jit(solution)/shard_map/ppermute | solution.py:14
  166.9 56.4 %collective-permute-start.3 = (f32[2560,128]{0,1:T(8,128)S(1)}, f32[2560,128]{0,1:T(8,128)S(1)}, u32[]{:S(2)}, u32[]{:S(2)}) collective-permute-start(f32[2560,128]{0,1:T(8,128)S(1)} %get-tuple-element.20), channel_id=1, source_target_pairs={{4,0},{8,4},{12,8},{16,12},{20,16},{24,20},{28,24},{5,1},{9,5},{13... | collective-permute-start | bytes 3932168 | tf_op jit(solution)/shard_map/ppermute | solution.py:14
  226.2 120.4 %all-gather.15.cloned.1.call-start = ((), (), s32[]{:S(2)}) async-start(), calls=%async_computation.3 | async-start | bytes 1310720 | tf_op jit(solution)/shard_map/all_gather | solution.py:67
  266.0 59.9 %collective-permute-start.4 = (f32[2560,128]{0,1:T(8,128)S(1)}, f32[2560,128]{0,1:T(8,128)S(1)}, u32[]{:S(2)}, u32[]{:S(2)}) collective-permute-start(f32[2560,128]{0,1:T(8,128)S(1)} %get-tuple-element.15), channel_id=1, source_target_pairs={{0,4},{4,8},{8,12},{12,16},{16,20},{20,24},{24,28},{1,5},{5,9},{9,... | collective-permute-start | bytes 3932168 | tf_op jit(solution)/shard_map/ppermute | solution.py:14
  269.5 56.4 %collective-permute-start.5 = (f32[2560,128]{0,1:T(8,128)S(1)}, f32[2560,128]{0,1:T(8,128)S(1)}, u32[]{:S(2)}, u32[]{:S(2)}) collective-permute-start(f32[2560,128]{0,1:T(8,128)S(1)} %get-tuple-element.16), channel_id=1, source_target_pairs={{4,0},{8,4},{12,8},{16,12},{20,16},{24,20},{28,24},{5,1},{9,5},{13... | collective-permute-start | bytes 3932168 | tf_op jit(solution)/shard_map/ppermute | solution.py:14
Sparse Core Ops, SparseCore 0:
  13.8 19.4 all-gather.8
  123.3 18.1 all-gather.10
  226.3 17.7 all-gather.12
  328.9 17.7 all-gather.14
